TPU v7x, 256 devices: a whole 4x4x8 slice. The times are simulated.
256 devices in a mesh: dp: 8 (over z_lo, core), mp: 16 (over x, y), group: 2 (over z_hi).
Axes of the slice: x: 4, y: 4, z: 8 (z_hi: 2, z_lo: 4; z = z_hi * 4 + z_lo), core: 2. Of those that a mesh axis runs over, the one named last changes fastest.
Arguments:
- hidden: bfloat16 [1024, 8192], P('dp', 'mp'), may hold values from -6 to 6
- neighbour_ids: int32 [16, 2, 128], P('dp', 'group'), may hold values from 0 to 65535, as said below
- counts: int32 [16], P('dp'), may hold values from 0 to 2
- embed_table: bfloat16 [65536, 8192], P(('dp', 'group'), 'mp'), may hold values from -6 to 6
- w_query: bfloat16 [8192, 4096], P('group', 'mp'), may hold values from -0.0625 to 0.0625
- w_key: bfloat16 [8192, 4096], P('group', 'mp'), may hold values from -0.0625 to 0.0625
- w_value: bfloat16 [8192, 4096], P('group', 'mp'), may hold values from -0.0625 to 0.0625
- w_out: bfloat16 [4096, 8192], P('mp', 'group'), may hold values from -0.09375 to 0.09375
- grad_out: bfloat16 [1024, 8192], P('dp', 'mp'), may hold values from -6 to 6
Outputs:
- output: float32 [1024, 8192], P('dp', 'mp')
- grad_hidden: float32 [1024, 8192], P('dp', 'mp')
- grad_neighbours: float32 [16, 2, 128, 8192], P('dp', 'group', None, 'mp')
Inputs may be any that keep to these rules, and one draw needn't show every extreme that they name: `neighbour_ids`: token ids of the retrieved neighbours; the ids are split into 16 owners of 4096 consecutive ids each; of the 256 ids of one window's neighbour k (blocks of one window, one k), at most 64 belong to one owner, and exactly 64 belong to some owner. neighbours k < counts[c] of block c are used, the others are masked.
All inputs are finite; a program needn't handle non-finite values.
Results may differ from a plain program's by a relative error of at most 0.019.
Values may be sent and summed in bfloat16 or wider, within the bound.
A program may use at most 128 MiB of HBM per device.

v0:
```python
import math
import jax
import jax.numpy as jnp
from jax import lax
from jax.sharding import PartitionSpec as P

HD = 128
BLOCK = 64
RET = 128


def contract(left, right):
    return lax.dot_general(
        left, right, (((1,), (1,)), ((), ())), preferred_element_type=jnp.float32
    )


def per_device(
    hidden, neighbour_ids, counts, embed_table, w_query, w_key, w_value, w_out, grad_out
):
    tail_rows = BLOCK - 1
    rows_here = hidden.shape[0]
    blocks_here = rows_here // BLOCK
    heads_here = w_query.shape[1] // HD
    inv_root = 1.0 / math.sqrt(HD)
    keep_rows = rows_here - tail_rows
    pad_rows = jnp.zeros((tail_rows, hidden.shape[1]), jnp.bfloat16)
    query_rows = jnp.concatenate([hidden[tail_rows:], pad_rows], 0)
    grad_rows = jnp.concatenate([grad_out[tail_rows:], pad_rows], 0)
    full_query, full_grad = (
        lax.all_gather(query_rows, "mp", axis=1, tiled=True),
        lax.all_gather(grad_rows, "mp", axis=1, tiled=True),
    )
    flat_ids = neighbour_ids.reshape(-1)
    block_rows = embed_table.shape[0]
    owners = lax.axis_size("dp") * lax.axis_size("group")
    cap = flat_ids.shape[0] // 4
    every_id = (
        lax.all_gather(flat_ids.astype(jnp.float32), ("dp", "group"), axis=0, tiled=True)
        .astype(jnp.int32)
        .reshape(owners, -1)
    )
    owner = lax.axis_index("dp") * lax.axis_size("group") + lax.axis_index("group")
    local_ids = every_id - owner * block_rows
    inside = (local_ids >= 0) & (local_ids < block_rows)
    rank = jnp.cumsum(inside.astype(jnp.int32), axis=1) - 1
    slot_hit = inside[:, :, None] & (rank[:, :, None] == jnp.arange(cap)[None, None, :])
    send_rows = jnp.sum(jnp.where(slot_hit, local_ids[:, :, None], 0), axis=1)
    send_buf = embed_table[send_rows.reshape(-1)].reshape(owners, cap, -1)
    recv_buf = lax.all_to_all(send_buf, ("dp", "group"), 0, 0, tiled=True)
    own_owner = flat_ids // block_rows
    same_owner = own_owner[:, None] == jnp.arange(owners)[None, :]
    own_rank = (
        jnp.sum(jnp.where(same_owner, jnp.cumsum(same_owner.astype(jnp.int32), axis=0), 0), axis=1)
        - 1
    )
    own_cols = recv_buf.reshape(owners * cap, -1)[own_owner * cap + own_rank]
    neighbours = lax.all_gather(own_cols, "mp", axis=1, tiled=True)
    wq_full, wk_full, wv_full = (
        lax.all_gather(w_query, "group", axis=0, tiled=True),
        lax.all_gather(w_key, "group", axis=0, tiled=True),
        lax.all_gather(w_value, "group", axis=0, tiled=True),
    )
    query_sum = jnp.dot(full_query, wq_full, preferred_element_type=jnp.float32)
    query = query_sum.astype(jnp.bfloat16)
    wo_full = lax.all_gather(w_out, "group", axis=1, tiled=True)
    keys = jnp.dot(neighbours, wk_full, preferred_element_type=jnp.float32).astype(jnp.bfloat16)
    values = jnp.dot(neighbours, wv_full, preferred_element_type=jnp.float32).astype(jnp.bfloat16)
    key_block = keys.reshape(blocks_here, RET, heads_here, HD)
    value_block = values.reshape(blocks_here, RET, heads_here, HD)
    query_block = query.reshape(blocks_here, BLOCK, heads_here, HD)
    live = (counts > lax.axis_index("group")).astype(jnp.float32)
    scores = (
        jnp.einsum("cqhd,ckhd->chqk", query_block, key_block, preferred_element_type=jnp.float32)
        * inv_root
    )
    weights = jnp.exp(scores) * live[:, None, None, None]
    numer = jnp.einsum(
        "chqk,ckhd->cqhd",
        weights.astype(jnp.bfloat16),
        value_block,
        preferred_element_type=jnp.float32,
    )
    partial_total = jnp.sum(weights, -1)
    numer, partial_total = lax.psum((numer, partial_total), "group")
    total = partial_total + 1.0
    attn = numer / jnp.transpose(total, (0, 2, 1))[..., None]
    attn_bf = attn.reshape(rows_here, heads_here * HD).astype(jnp.bfloat16)
    out_term = jnp.dot(attn_bf, wo_full, preferred_element_type=jnp.float32)
    d_attn = contract(full_grad, wo_full).astype(jnp.bfloat16)
    d_block = d_attn.reshape(blocks_here, BLOCK, heads_here, HD)
    prob = weights / total[..., None]
    d_prob = jnp.einsum("cqhd,ckhd->chqk", d_block, value_block, preferred_element_type=jnp.float32)
    delta = jnp.sum(d_block.astype(jnp.float32) * attn, -1)
    d_score = (prob * (d_prob - jnp.transpose(delta, (0, 2, 1))[..., None])).astype(jnp.bfloat16)
    query_part = jnp.einsum(
        "chqk,ckhd->cqhd", d_score, key_block, preferred_element_type=jnp.float32
    )
    query_grad = lax.psum(query_part, "group")
    d_query = (query_grad * inv_root).astype(jnp.bfloat16).reshape(rows_here, heads_here * HD)
    d_keys = (
        jnp.einsum("chqk,cqhd->ckhd", d_score, query_block, preferred_element_type=jnp.float32)
        * inv_root
    ).astype(jnp.bfloat16)
    d_values = jnp.einsum(
        "chqk,cqhd->ckhd", prob.astype(jnp.bfloat16), d_block, preferred_element_type=jnp.float32
    ).astype(jnp.bfloat16)
    d_keys = d_keys.reshape(blocks_here * RET, heads_here * HD)
    d_values = d_values.reshape(blocks_here * RET, heads_here * HD)
    hid_term = contract(d_query, wq_full)
    out_cols, hid_cols = (
        lax.psum_scatter(
            out_term.astype(jnp.bfloat16), "mp", scatter_dimension=1, tiled=True
        ).astype(jnp.float32),
        lax.psum_scatter(
            hid_term.astype(jnp.bfloat16), "mp", scatter_dimension=1, tiled=True
        ).astype(jnp.float32),
    )
    zero_rows = jnp.zeros((tail_rows, out_cols.shape[1]), jnp.float32)
    output = jnp.concatenate([zero_rows, out_cols[:keep_rows]], 0)
    grad_hidden = jnp.concatenate([zero_rows, hid_cols[:keep_rows]], 0)
    neigh_term = contract(d_keys, wk_full) + contract(d_values, wv_full)
    neigh_cols = lax.psum_scatter(
        neigh_term.astype(jnp.bfloat16), "mp", scatter_dimension=1, tiled=True
    ).astype(jnp.float32)
    grad_neighbours = neigh_cols.reshape(blocks_here, 1, RET, neigh_cols.shape[1])
    return (output, grad_hidden, grad_neighbours)


def solution(mesh):
    return jax.shard_map(
        per_device,
        mesh=mesh,
        in_specs=(
            P("dp", "mp"),
            P("dp", "group", None),
            P("dp"),
            P(("dp", "group"), "mp"),
            P("group", "mp"),
            P("group", "mp"),
            P("group", "mp"),
            P("mp", "group"),
            P("dp", "mp"),
        ),
        out_specs=(P("dp", "mp"), P("dp", "mp"), P("dp", "group", None, "mp")),
        check_vma=False,
    )
```

profile of v0, /device:TPU:2, one launch (start us, length us, event | category | flops | bytes accessed | tf_op | source)
XLA Modules:
  0.0 972.8 jit_solution(12286093274936307989)
XLA Ops:
  7.2 0.9 slice.30
  9.6 0.9 slice.32
  12.4 40.9 %all-gather.1 = f32[16,1,256]{2,1,0:T(1,128)S(1)} all-gather(f32[1,1,256]{2,1,0:T(1,128)S(1)} %bitcast.107), channel_id=1, replica_groups=mesh['dp'=8,'mp'=16,'group'=2] {'dp','group'}, dimensions={0}, use_global_device_ids=true | all-gather | bytes 17408 | tf_op jit(solution)/shard_map/all_gather | solution.py:39
  54.8 7.9 gather_fusion
  62.7 6.0 all-to-all-start
  69.8 38.2 %all-to-all-done = bf16[16,64,512]{2,1,0:T(8,128)(2,1)S(1)} async-done(((bf16[16,64,512]{2,1,0:T(8,128)(2,1)}), bf16[16,64,512]{2,1,0:T(8,128)(2,1)S(1)}, u32[]{:S(2)}, u32[]{:S(2)}) %all-to-all-start) | async-done | bytes 1048608 | tf_op jit(solution)/shard_map/all_to_all | solution.py:50
  107.9 1.9 gather_fusion.1
  110.7 60.2 %all-gather.14.cloned.1.call-done = bf16[8192,256]{1,0:T(8,128)(2,1)} async-done(((bf16[4096,256]{1,0:T(8,128)(2,1)}), bf16[8192,256]{1,0:T(8,128)(2,1)}) %all-gather.14.cloned.1.call-update) | async-done | bytes 4194320 | tf_op jit(solution)/shard_map/all_gather | solution.py:60
  170.9 3.5 convolution_convert_fusion.6
  174.4 65.6 %all-gather.20.cloned.1.call-done = bf16[128,8192]{1,0:T(8,128)(2,1)} async-done(((bf16[128,512]{1,0:T(8,128)(2,1)}), bf16[128,8192]{1,0:T(8,128)(2,1)}) %all-gather.20.cloned.1.call-update) | async-done | bytes 2097168 | tf_op jit(solution)/shard_map/all_gather | solution.py:32
  240.0 113.4 %all-gather.18.cloned.1.call-done = bf16[256,8192]{1,0:T(8,128)(2,1)} async-done(((bf16[256,4096]{1,0:T(8,128)(2,1)}), bf16[256,8192]{1,0:T(8,128)(2,1)}) %all-gather.18.cloned.1.call-update) | async-done | bytes 4194320 | tf_op jit(solution)/shard_map/all_gather | solution.py:66
  353.4 4.4 convolution_convert_fusion.5
  357.8 105.4 %all-gather.10.cloned.1.call-done = bf16[8192,256]{1,0:T(8,128)(2,1)} async-done(((bf16[4096,256]{1,0:T(8,128)(2,1)}), bf16[8192,256]{1,0:T(8,128)(2,1)}) %all-gather.10.cloned.1.call-update) | async-done | bytes 4194320 | tf_op jit(solution)/shard_map/all_gather | solution.py:62
  463.2 61.3 %all-gather.22.cloned.1.call-done = bf16[256,8192]{1,0:T(8,128)(2,1)} async-done(((bf16[256,512]{1,0:T(8,128)(2,1)}), bf16[256,8192]{1,0:T(8,128)(2,1)}) %all-gather.22.cloned.1.call-update) | async-done | bytes 4194320 | tf_op jit(solution)/shard_map/all_gather | solution.py:58
  524.5 4.7 convolution_convert_fusion.4
  529.2 108.8 %all-gather.16.cloned.1.call-done = bf16[8192,256]{1,0:T(8,128)(2,1)} async-done(((bf16[4096,256]{1,0:T(8,128)(2,1)}), bf16[8192,256]{1,0:T(8,128)(2,1)}) %all-gather.16.cloned.1.call-update) | async-done | bytes 4194320 | tf_op jit(solution)/shard_map/all_gather | solution.py:61
  638.1 4.7 convolution_convert_fusion.3
  644.0 8.8 psum.22
  652.9 25.8 %all-reduce.7.cloned.1.call-done = f32[2,64,2,128]{3,1,2,0:T(8,128)} async-done(((f32[2,64,2,128]{3,1,2,0:T(8,128)}), f32[2,64,2,128]{3,1,2,0:T(8,128)}) %all-reduce.7.cloned.1.call-update) | async-done | bytes 131088 | tf_op jit(solution)/shard_map/psum | solution.py:85
  678.7 1.1 multiply_reduce_fusion
  681.0 4.3 convolution_convert_fusion.1
  685.3 31.5 %all-reduce.9.cloned.1.call-done = f32[2,64,2,128]{3,1,2,0:T(8,128)} async-done(((f32[2,64,2,128]{3,1,2,0:T(8,128)}), f32[2,64,2,128]{3,1,2,0:T(8,128)}) %all-reduce.9.cloned.1.call-update) | async-done | bytes 131088 | tf_op jit(solution)/shard_map/psum | solution.py:99
  716.9 0.9 multiply_convert_fusion
  717.9 5.0 convolution_convert_fusion
  724.0 3.6 fusion.11
  727.6 3.2 fusion
  730.8 64.9 %reduce-scatter.4.cloned.1.call-done = bf16[128,512]{1,0:T(8,128)(2,1)} async-done(((bf16[128,8192]{1,0:T(8,128)(2,1)}), bf16[128,512]{1,0:T(8,128)(2,1)}) %reduce-scatter.4.cloned.1.call-update) | async-done | bytes 131088 | tf_op jit(solution)/shard_map/reduce_scatter | solution.py:112
  795.7 0.9 slice.40
  797.3 81.1 %reduce-scatter.6.cloned.1.call-done = bf16[128,512]{1,0:T(8,128)(2,1)} async-done(((bf16[128,8192]{1,0:T(8,128)(2,1)}), bf16[128,512]{1,0:T(8,128)(2,1)}) %reduce-scatter.6.cloned.1.call-update) | async-done | bytes 131088 | tf_op jit(solution)/shard_map/reduce_scatter | solution.py:115
  878.5 0.9 slice.41
  880.1 84.0 %reduce-scatter.8.cloned.1.call-done = bf16[256,512]{1,0:T(8,128)(2,1)} async-done(((bf16[256,8192]{1,0:T(8,128)(2,1)}), bf16[256,512]{1,0:T(8,128)(2,1)}) %reduce-scatter.8.cloned.1.call-update) | async-done | bytes 262160 | tf_op jit(solution)/shard_map/reduce_scatter | solution.py:123
  964.1 1.8 convert.9
  (78 shorter events, 11.6 us)
Async XLA Ops:
  7.2 5.2 copy-start.1
  7.2 103.5 %all-gather.12.cloned.1.call-start = ((), (), s32[]{:S(2)}) async-start(), calls=%async_computation.5 | async-start | bytes 2228224 | tf_op jit(solution)/shard_map/all_gather | solution.py:31
  8.8 162.1 %all-gather.14.cloned.1.call-start = ((), (), s32[]{:S(2)}) async-start(), calls=%async_computation.6 | async-start | bytes 6291456 | tf_op jit(solution)/shard_map/all_gather | solution.py:60
  9.6 230.4 %all-gather.20.cloned.1.call-start = ((), (), s32[]{:S(2)}) async-start(), calls=%async_computation.11 | async-start | bytes 2228224 | tf_op jit(solution)/shard_map/all_gather | solution.py:32
  11.2 342.2 %all-gather.18.cloned.1.call-start = ((), (), s32[]{:S(2)}) async-start(), calls=%async_computation.9 | async-start | bytes 6291456 | tf_op jit(solution)/shard_map/all_gather | solution.py:66
  11.8 451.4 %all-gather.10.cloned.1.call-start = ((), (), s32[]{:S(2)}) async-start(), calls=%async_computation.4 | async-start | bytes 6291456 | tf_op jit(solution)/shard_map/all_gather | solution.py:62
  62.7 47.9 %copy-start.2 = (s32[2]{0:T(128)S(1)}, s32[2]{0:T(128)}, u32[]{:S(2)}) copy-start(s32[2]{0:T(128)} %param.11) | copy-start | bytes 28
  62.7 45.2 %all-to-all-start = ((bf16[16,64,512]{2,1,0:T(8,128)(2,1)}), bf16[16,64,512]{2,1,0:T(8,128)(2,1)S(1)}, u32[]{:S(2)}, u32[]{:S(2)}) async-start(bf16[16,64,512]{2,1,0:T(8,128)(2,1)} %bitcast.4), calls=%async_computation | async-start | bytes 2097152 | tf_op jit(solution)/shard_map/all_to_all | solution.py:50
  68.7 455.8 %all-gather.22.cloned.1.call-start = ((), (), s32[]{:S(2)}) async-start(), calls=%async_computation.15 | async-start | bytes 4456448 | tf_op jit(solution)/shard_map/all_gather | solution.py:58
  109.8 528.2 %all-gather.16.cloned.1.call-start = ((), (), s32[]{:S(2)}) async-start(), calls=%async_computation.7 | async-start | bytes 6291456 | tf_op jit(solution)/shard_map/all_gather | solution.py:61
  110.6 568.1 %all-reduce.7.cloned.1.call-start = ((), (), s32[]{:S(2)}) async-start(), calls=%async_computation.8 | async-start | bytes 262144 | tf_op jit(solution)/shard_map/psum | solution.py:85
  644.0 72.9 %all-reduce.9.cloned.1.call-start = ((), (), s32[]{:S(2)}) async-start(), calls=%async_computation.12 | async-start | bytes 262144 | tf_op jit(solution)/shard_map/psum | solution.py:99
  680.9 114.8 %reduce-scatter.4.cloned.1.call-start = ((), (), s32[]{:S(2)}) async-start(), calls=%async_computation.10 | async-start | bytes 2228224 | tf_op jit(solution)/shard_map/reduce_scatter | solution.py:112
  685.3 193.2 %reduce-scatter.6.cloned.1.call-start = ((), (), s32[]{:S(2)}) async-start(), calls=%async_computation.13 | async-start | bytes 2228224 | tf_op jit(solution)/shard_map/reduce_scatter | solution.py:115
  722.9 241.2 %reduce-scatter.8.cloned.1.call-start = ((), (), s32[]{:S(2)}) async-start(), calls=%async_computation.14 | async-start | bytes 4456448 | tf_op jit(solution)/shard_map/reduce_scatter | solution.py:123
  723.9 3.6 copy-start
Sparse Core Ops, SparseCore 0:
  11.0 55.3 all-gather.11
  68.1 102.6 all-gather.13
  173.9 66.1 all-gather.19
  241.7 111.7 all-gather.17
  355.1 108.0 all-gather.9
  466.1 58.3 all-gather.21
  526.3 111.7 all-gather.15
  644.1 34.5 all-reduce.6
  681.9 34.9 all-reduce.8
  720.3 75.4 reduce-scatter.3
  799.7 78.6 reduce-scatter.5
  881.9 82.1 reduce-scatter.7
where the time goes:
time: 973 us
  waiting for transfers between devices  843 us (87%)
  blocking collectives  49.7 us (5%)
  matrix products  36.1 us (4%)
  local copies, waits for them, and re-layouts  15.7 us (2%)
  between operations  14.5 us (1%)
    all_gather x1, waiting for transfers between devices, per_device(): wo_full = lax.all_gather(w_out, 'group', axis=1, tiled=True)  113 us
    all_gather x1, waiting for transfers between devices, per_device(): lax.all_gather(w_key, 'group', axis=0, tiled=True)  109 us
    all_gather x1, waiting for transfers between devices, per_device(): lax.all_gather(w_value, 'group', axis=0, tiled=True)  105 us
    reduce_scatter x1, waiting for transfers between devices, per_device(): lax.psum_scatter(neigh_term.astype(jnp.bfloat16), 'mp', scatter_dimension...  84 us
    reduce_scatter x1, waiting for transfers between devices, per_device(): lax.psum_scatter(hid_term.astype(jnp.bfloat16), 'mp', scatter_dimension=1...  81.1 us
    all_gather x1, waiting for transfers between devices, per_device(): lax.all_gather(grad_rows, 'mp', axis=1, tiled=True)  65.6 us
    reduce_scatter x1, waiting for transfers between devices, per_device(): lax.psum_scatter(out_term.astype(jnp.bfloat16), 'mp', scatter_dimension=1...  64.9 us
    all_gather x1, waiting for transfers between devices, per_device(): neighbours = lax.all_gather(own_cols, 'mp', axis=1, tiled=True)  61.3 us
  transfers between devices with their start and end apart: 13, of which 12 were waited for; matrix products, arithmetic and copies ran while one was open for 5% of the time, Pallas kernels for 0%

commit v1 on v0

--- a/solution.py
+++ b/solution.py
@@ -63,7 +63,9 @@
     )
     query_sum = jnp.dot(full_query, wq_full, preferred_element_type=jnp.float32)
     query = query_sum.astype(jnp.bfloat16)
-    wo_full = lax.all_gather(w_out, "group", axis=1, tiled=True)
+    wo_full = jnp.concatenate(
+        lax.all_to_all(jnp.stack([w_out] * lax.axis_size("group")), "group", 0, 0), axis=1
+    )
     keys = jnp.dot(neighbours, wk_full, preferred_element_type=jnp.float32).astype(jnp.bfloat16)
     values = jnp.dot(neighbours, wv_full, preferred_element_type=jnp.float32).astype(jnp.bfloat16)
     key_block = keys.reshape(blocks_here, RET, heads_here, HD)

time: 973 us -> 940 us (0.966)
  waiting for transfers between devices: 843 us -> 799 us
    all_gather x1 -> x0, waiting for transfers between devices: 113 us -> none  [per_device(): wo_full = lax.all_gather(w_out, 'group', axis=1, tiled=True)]
    all_gather x1, waiting for transfers between devices: 65.6 us -> 123 us  [per_device(): lax.all_gather(grad_rows, 'mp', axis=1, tiled=True)]
    all_gather x1, waiting for transfers between devices: 60.2 us -> 70.2 us  [per_device(): lax.all_gather(w_query, 'group', axis=0, tiled=True)]
  transfers between devices with their start and end apart: 13 -> 13, of which waited for: 12 -> 11; matrix products, arithmetic and copies ran while one was open for 5% -> 6% of each run, Pallas kernels for 0% -> 0%
where the time goes in v1:
time: 940 us
  waiting for transfers between devices  799 us (85%)
  blocking collectives  49.7 us (5%)
  matrix products  36.1 us (4%)
  local copies, waits for them, and re-layouts  18.9 us (2%)
  between operations  14.2 us (2%)
  starting transfers between devices  12.4 us (1%)
  other arithmetic  9.53 us (1%)
    all_gather x1, waiting for transfers between devices, per_device(): lax.all_gather(grad_rows, 'mp', axis=1, tiled=True)  123 us
    all_gather x1, waiting for transfers between devices, per_device(): lax.all_gather(w_value, 'group', axis=0, tiled=True)  110 us
    all_gather x1, waiting for transfers between devices, per_device(): lax.all_gather(w_key, 'group', axis=0, tiled=True)  109 us
    reduce_scatter x1, waiting for transfers between devices, per_device(): lax.psum_scatter(neigh_term.astype(jnp.bfloat16), 'mp', scatter_dimension...  84.2 us
    reduce_scatter x1, waiting for transfers between devices, per_device(): lax.psum_scatter(hid_term.astype(jnp.bfloat16), 'mp', scatter_dimension=1...  81 us
    all_gather x1, waiting for transfers between devices, per_device(): lax.all_gather(w_query, 'group', axis=0, tiled=True)  70.2 us
    reduce_scatter x1, waiting for transfers between devices, per_device(): lax.psum_scatter(out_term.astype(jnp.bfloat16), 'mp', scatter_dimension=1...  65 us
    all_gather x1, waiting for transfers between devices, per_device(): neighbours = lax.all_gather(own_cols, 'mp', axis=1, tiled=True)  61.3 us
  transfers between devices with their start and end apart: 13, of which 11 were waited for; matrix products, arithmetic and copies ran while one was open for 6% of the time, Pallas kernels for 0%

profile of v1, /device:TPU:2, one launch (start us, length us, event | category | flops | bytes accessed | tf_op | source)
XLA Modules:
  0.0 939.7 jit_solution(14721480694538555153)
XLA Ops:
  7.2 0.9 slice.30
  9.6 0.9 slice.32
  11.8 40.9 %all-gather.1 = f32[16,1,256]{2,1,0:T(1,128)S(1)} all-gather(f32[1,1,256]{2,1,0:T(1,128)S(1)} %bitcast.112), channel_id=1, replica_groups=mesh['dp'=8,'mp'=16,'group'=2] {'dp','group'}, dimensions={0}, use_global_device_ids=true | all-gather | bytes 17408 | tf_op jit(solution)/shard_map/all_gather | solution.py:39
  54.2 7.8 gather_fusion
  62.1 6.0 all-to-all-start
  69.1 37.6 %all-to-all-done = bf16[16,64,512]{2,1,0:T(8,128)(2,1)S(1)} async-done(((bf16[16,64,512]{2,1,0:T(8,128)(2,1)}), bf16[16,64,512]{2,1,0:T(8,128)(2,1)S(1)}, u32[]{:S(2)}, u32[]{:S(2)}) %all-to-all-start) | async-done | bytes 1048608 | tf_op jit(solution)/shard_map/all_to_all | solution.py:50
  106.7 1.9 gather_fusion.1
  108.6 3.3 copy.62
  111.9 2.3 pad_maximum_fusion
  114.2 5.9 all-to-all-start.1
  120.7 70.2 %all-gather.13.cloned.1.call-done = bf16[8192,256]{1,0:T(8,128)(2,1)} async-done(((bf16[4096,256]{1,0:T(8,128)(2,1)}), bf16[8192,256]{1,0:T(8,128)(2,1)}) %all-gather.13.cloned.1.call-update) | async-done | bytes 4194320 | tf_op jit(solution)/shard_map/all_gather | solution.py:60
  190.9 3.5 convolution_convert_fusion.6
  194.5 122.6 %all-gather.17.cloned.1.call-done = bf16[128,8192]{1,0:T(8,128)(2,1)} async-done(((bf16[128,512]{1,0:T(8,128)(2,1)}), bf16[128,8192]{1,0:T(8,128)(2,1)}) %all-gather.17.cloned.1.call-update) | async-done | bytes 2097168 | tf_op jit(solution)/shard_map/all_gather | solution.py:32
  317.1 3.5 convolution_convert_fusion.5
  320.7 109.9 %all-gather.9.cloned.1.call-done = bf16[8192,256]{1,0:T(8,128)(2,1)} async-done(((bf16[4096,256]{1,0:T(8,128)(2,1)}), bf16[8192,256]{1,0:T(8,128)(2,1)}) %all-gather.9.cloned.1.call-update) | async-done | bytes 4194320 | tf_op jit(solution)/shard_map/all_gather | solution.py:62
  430.6 61.3 %all-gather.19.cloned.1.call-done = bf16[256,8192]{1,0:T(8,128)(2,1)} async-done(((bf16[256,512]{1,0:T(8,128)(2,1)}), bf16[256,8192]{1,0:T(8,128)(2,1)}) %all-gather.19.cloned.1.call-update) | async-done | bytes 4194320 | tf_op jit(solution)/shard_map/all_gather | solution.py:58
  491.8 4.7 convolution_convert_fusion.4
  496.6 108.7 %all-gather.15.cloned.1.call-done = bf16[8192,256]{1,0:T(8,128)(2,1)} async-done(((bf16[4096,256]{1,0:T(8,128)(2,1)}), bf16[8192,256]{1,0:T(8,128)(2,1)}) %all-gather.15.cloned.1.call-update) | async-done | bytes 4194320 | tf_op jit(solution)/shard_map/all_gather | solution.py:61
  605.2 4.7 convolution_convert_fusion.3
  611.2 8.8 psum.22
  620.0 25.8 %all-reduce.7.cloned.1.call-done = f32[2,64,2,128]{3,1,2,0:T(8,128)} async-done(((f32[2,64,2,128]{3,1,2,0:T(8,128)}), f32[2,64,2,128]{3,1,2,0:T(8,128)}) %all-reduce.7.cloned.1.call-update) | async-done | bytes 131088 | tf_op jit(solution)/shard_map/psum | solution.py:87
  645.9 1.1 multiply_reduce_fusion
  648.2 5.0 convolution_convert_fusion.1
  653.3 30.7 %all-reduce.9.cloned.1.call-done = f32[2,64,2,128]{3,1,2,0:T(8,128)} async-done(((f32[2,64,2,128]{3,1,2,0:T(8,128)}), f32[2,64,2,128]{3,1,2,0:T(8,128)}) %all-reduce.9.cloned.1.call-update) | async-done | bytes 131088 | tf_op jit(solution)/shard_map/psum | solution.py:101
  684.0 0.9 multiply_convert_fusion
  685.0 5.0 convolution_convert_fusion
  691.1 3.6 fusion.11
  694.8 3.2 fusion
  698.0 65.0 %reduce-scatter.4.cloned.1.call-done = bf16[128,512]{1,0:T(8,128)(2,1)} async-done(((bf16[128,8192]{1,0:T(8,128)(2,1)}), bf16[128,512]{1,0:T(8,128)(2,1)}) %reduce-scatter.4.cloned.1.call-update) | async-done | bytes 131088 | tf_op jit(solution)/shard_map/reduce_scatter | solution.py:114
  764.7 81.0 %reduce-scatter.6.cloned.1.call-done = bf16[128,512]{1,0:T(8,128)(2,1)} async-done(((bf16[128,8192]{1,0:T(8,128)(2,1)}), bf16[128,512]{1,0:T(8,128)(2,1)}) %reduce-scatter.6.cloned.1.call-update) | async-done | bytes 131088 | tf_op jit(solution)/shard_map/reduce_scatter | solution.py:117
  847.2 84.2 %reduce-scatter.8.cloned.1.call-done = bf16[256,512]{1,0:T(8,128)(2,1)} async-done(((bf16[256,8192]{1,0:T(8,128)(2,1)}), bf16[256,512]{1,0:T(8,128)(2,1)}) %reduce-scatter.8.cloned.1.call-update) | async-done | bytes 262160 | tf_op jit(solution)/shard_map/reduce_scatter | solution.py:125
  931.4 1.8 convert.9
  (79 shorter events, 12.7 us)
Async XLA Ops:
  7.2 4.6 copy-start.1
  7.2 113.6 %all-gather.11.cloned.1.call-start = ((), (), s32[]{:S(2)}) async-start(), calls=%async_computation.6 | async-start | bytes 2228224 | tf_op jit(solution)/shard_map/all_gather | solution.py:31
  8.8 182.1 %all-gather.13.cloned.1.call-start = ((), (), s32[]{:S(2)}) async-start(), calls=%async_computation.7 | async-start | bytes 6291456 | tf_op jit(solution)/shard_map/all_gather | solution.py:60
  9.6 307.6 %all-gather.17.cloned.1.call-start = ((), (), s32[]{:S(2)}) async-start(), calls=%async_computation.11 | async-start | bytes 2228224 | tf_op jit(solution)/shard_map/all_gather | solution.py:32
  11.2 419.3 %all-gather.9.cloned.1.call-start = ((), (), s32[]{:S(2)}) async-start(), calls=%async_computation.5 | async-start | bytes 6291456 | tf_op jit(solution)/shard_map/all_gather | solution.py:62
  62.1 44.6 %all-to-all-start = ((bf16[16,64,512]{2,1,0:T(8,128)(2,1)}), bf16[16,64,512]{2,1,0:T(8,128)(2,1)S(1)}, u32[]{:S(2)}, u32[]{:S(2)}) async-start(bf16[16,64,512]{2,1,0:T(8,128)(2,1)} %bitcast.4), calls=%async_computation | async-start | bytes 2097152 | tf_op jit(solution)/shard_map/all_to_all | solution.py:50
  68.1 423.7 %all-gather.19.cloned.1.call-start = ((), (), s32[]{:S(2)}) async-start(), calls=%async_computation.15 | async-start | bytes 4456448 | tf_op jit(solution)/shard_map/all_gather | solution.py:58
  114.2 6.5 copy-start.2
  114.2 202.9 %all-to-all-start.1 = ((bf16[2,256,4096]{1,2,0:T(8,128)(2,1)}), bf16[2,256,4096]{1,2,0:T(8,128)(2,1)}, u32[]{:S(2)}, u32[]{:S(2)}) async-start(bf16[2,256,4096]{1,2,0:T(8,128)(2,1)} %pad_maximum_fusion), calls=%async_computation.1 | async-start | bytes 8388608 | tf_op jit(solution)/shard_map/all_to_all | solution.py:67
  120.1 485.1 %all-gather.15.cloned.1.call-start = ((), (), s32[]{:S(2)}) async-start(), calls=%async_computation.8 | async-start | bytes 6291456 | tf_op jit(solution)/shard_map/all_gather | solution.py:61
  120.6 525.2 %all-reduce.7.cloned.1.call-start = ((), (), s32[]{:S(2)}) async-start(), calls=%async_computation.9 | async-start | bytes 262144 | tf_op jit(solution)/shard_map/psum | solution.py:87
  611.1 72.9 %all-reduce.9.cloned.1.call-start = ((), (), s32[]{:S(2)}) async-start(), calls=%async_computation.12 | async-start | bytes 262144 | tf_op jit(solution)/shard_map/psum | solution.py:101
  648.1 114.9 %reduce-scatter.4.cloned.1.call-start = ((), (), s32[]{:S(2)}) async-start(), calls=%async_computation.10 | async-start | bytes 2228224 | tf_op jit(solution)/shard_map/reduce_scatter | solution.py:114
  653.2 192.4 %reduce-scatter.6.cloned.1.call-start = ((), (), s32[]{:S(2)}) async-start(), calls=%async_computation.13 | async-start | bytes 2228224 | tf_op jit(solution)/shard_map/reduce_scatter | solution.py:117
  690.1 241.3 %reduce-scatter.8.cloned.1.call-start = ((), (), s32[]{:S(2)}) async-start(), calls=%async_computation.14 | async-start | bytes 4456448 | tf_op jit(solution)/shard_map/reduce_scatter | solution.py:125
  691.1 3.6 copy-start
Sparse Core Ops, SparseCore 0:
  11.0 55.3 all-gather.10
  68.1 122.7 all-gather.12
  193.9 123.1 all-gather.16
  318.8 111.7 all-gather.8
  433.4 58.3 all-gather.18
  493.5 111.7 all-gather.14
  611.3 34.5 all-reduce.6
  649.0 34.9 all-reduce.8
  687.6 75.4 reduce-scatter.3
  766.9 78.6 reduce-scatter.5
  849.3 82.0 reduce-scatter.7
